TPU v7x, 256 devices: a whole 4x4x8 slice. The times are simulated.
256 devices in a mesh: tok: 16 (over y, x), ch: 16 (over z, core).
Axes of the slice: x: 4, y: 4, z: 8, core: 2. Of those that a mesh axis runs over, the one named last changes fastest.
Arguments:
- tokens: bfloat16 [256, 16384], P('tok', 'ch'), may hold values from -64 to 64
- probe: int32 [256, 16384], P('tok', 'ch'), may hold values from 0 to 1
- signs: int32 [16384], P('ch'), may hold values from 0 to 1
- gate_weight: bfloat16 [16384, 26624], P('ch', 'tok'), may hold values from -0.046875 to 0.046875
- up_weight: bfloat16 [16384, 26624], P('ch', 'tok'), may hold values from -0.046875 to 0.046875
- down_weight: bfloat16 [26624, 16384], P('tok', 'ch'), may hold values from -0.0390625 to 0.0390625
Outputs:
- rotated_product: float32 [256, 16384], P('tok', 'ch')
- diagonal_estimate: float32 [16384], P('ch')
All inputs are finite; a program needn't handle non-finite values.
Results may differ from a plain program's by a relative error of at most 0.004.
Values may be sent and summed in bfloat16 or wider, within the bound.
No kernel may reach another device: no remote copies, remote signals or barrier semaphores. Data moves between devices by JAX's collectives and lax.ppermute only.
A program may use at most 128 MiB of HBM per device.

v0:
```python
import math
import jax
import jax.numpy as jnp
import numpy as np
from jax import lax
from jax.sharding import PartitionSpec as P

D = 16384
LANES = 128
F32 = jnp.float32
BF16 = jnp.bfloat16


def sign_table(length):
    table = np.ones((1, 1), np.float32)
    while table.shape[0] < length:
        table = np.block([[table, table], [table, -table]])
    return table


def swap(value, mask):
    pairs = [(source, source ^ mask) for source in range(lax.axis_size("ch"))]
    return lax.ppermute(value, "ch", pairs)


def cross(values, my_index):
    for bit_pos in range(lax.axis_size("ch").bit_length() - 1):
        partner = swap(values, 2**bit_pos)
        upper = my_index >> bit_pos & 1 == 1
        values = jnp.where(upper, partner - values, values + partner)
    return values


def local_transform(values, table, precision=None):
    rows, length = values.shape
    groups = [values[:, at : at + LANES] for at in range(0, length, LANES)]
    step = 1
    while step < len(groups):
        for low in range(len(groups)):
            if not low & step:
                first, second = (groups[low], groups[low + step])
                groups[low], groups[low + step] = (first + second, first - second)
        step *= 2
    stacked = jnp.concatenate(groups, axis=0)
    done = jnp.dot(
        stacked, table.astype(values.dtype), precision=precision, preferred_element_type=F32
    )
    return jnp.concatenate([done[at : at + rows] for at in range(0, done.shape[0], rows)], axis=1)


def gather_tok(value):
    size = lax.axis_size("tok")
    copies = jnp.broadcast_to(value[None], (size,) + value.shape)
    return lax.all_to_all(copies, "tok", 0, 0, tiled=True)


def scatter_tok(value, send_type):
    size = lax.axis_size("tok")
    blocks = value.astype(send_type).reshape(size, value.shape[0] // size, value.shape[1])
    arrived = lax.all_to_all(blocks, "tok", 0, 0, tiled=True)
    return jnp.sum(arrived.astype(F32), axis=0)


def chip_groups():
    size = lax.axis_size("ch")
    return [[chip + core for chip in range(0, size, 2)] for core in range(2)]


def rows_of_core(value, core):
    size = lax.axis_size("ch")
    blocks = value.reshape(size // 2, 2, value.shape[0] // size, value.shape[1])
    chosen = lax.dynamic_index_in_dim(blocks, core, 1, keepdims=False)
    return chosen.reshape(value.shape[0] // 2, value.shape[1])


def scatter_ch(product, rows, core, swap_type, send_type):
    theirs = product(rows_of_core(rows, 1 - core)).astype(swap_type)
    arrived = swap(theirs, 1)
    mine = product(rows_of_core(rows, core))
    both = (mine + arrived.astype(F32)).astype(send_type)
    chips = lax.axis_size("ch") // 2
    blocks = both.reshape(chips, both.shape[0] // chips, both.shape[1])
    pieces = lax.all_to_all(blocks, "ch", 0, 0, tiled=True, axis_index_groups=chip_groups())
    return jnp.sum(pieces.astype(F32), axis=0)


def times(rows, weight):
    return jnp.dot(rows, weight, preferred_element_type=F32)


def times_t(rows, weight):
    return lax.dot_general(rows, weight, (((1,), (1,)), ((), ())), preferred_element_type=F32)


def on_device(tokens, probe, signs, gate_weight, up_weight, down_weight):
    tok_rows, channels = tokens.shape
    total_rows = tok_rows * lax.axis_size("tok")
    hidden = gate_weight.shape[1]
    my_index = lax.axis_index("ch")
    core = my_index & 1
    root_scale = 1.0 / math.sqrt(D)
    table = jnp.asarray(sign_table(LANES))
    probe_signs = (2 * probe - 1).astype(F32)
    channel_signs = (2 * signs - 1).astype(F32)
    all_tokens = gather_tok(tokens).reshape(total_rows, channels)
    token_part = jnp.stack([times(all_tokens, gate_weight), times(all_tokens, up_weight)], axis=1)
    token_sum = lax.psum_scatter(token_part, "ch", scatter_dimension=0, tiled=True)
    crossed = cross((probe_signs * channel_signs[None, :]).astype(BF16), my_index)
    tangent = (
        local_transform(crossed.astype(F32), table, lax.Precision.HIGHEST) * root_scale
    ).astype(BF16)
    all_tangent = gather_tok(tangent).reshape(total_rows, channels)

    def gate_and_up(rows):
        return jnp.concatenate([times(rows, gate_weight), times(rows, up_weight)], axis=1)

    tangent_sum = scatter_ch(gate_and_up, all_tangent, core, BF16, BF16)
    gate_pre, up_pre = (token_sum[:, 0], token_sum[:, 1])
    gate_tan, up_tan = (tangent_sum[:, :hidden], tangent_sum[:, hidden:])
    sigmoid_gate = jax.nn.sigmoid(gate_pre)
    activated = gate_pre * sigmoid_gate
    slope_term = sigmoid_gate * (1.0 + gate_pre * (1.0 - sigmoid_gate))
    hidden_tan = (slope_term * gate_tan * up_pre + activated * up_tan).astype(BF16)
    out_part = times(lax.all_gather(hidden_tan, "ch", axis=0, tiled=True), down_weight)
    out_tangent = scatter_tok(out_part, F32).astype(BF16)
    all_out = gather_tok(out_tangent).reshape(total_rows, channels)
    back_hidden = scatter_ch(lambda rows: times_t(rows, down_weight), all_out, core, F32, BF16)
    back_gate = (back_hidden * up_pre * slope_term).astype(BF16)
    back_up = (back_hidden * activated).astype(BF16)
    back = jnp.concatenate([back_gate, back_up], axis=1)
    mine = lax.all_gather(back, "ch", axis=0, tiled=True, axis_index_groups=chip_groups())
    theirs = swap(mine, 1)

    def grad(rows):
        return times_t(rows[:, :hidden], gate_weight) + times_t(rows[:, hidden:], up_weight)

    in_mine, in_theirs = (grad(mine), grad(theirs))
    split = (lax.axis_size("ch") // 2, tok_rows, channels)
    in_mine, in_theirs = (in_mine.reshape(split), in_theirs.reshape(split))
    first = core == 0
    in_part = jnp.stack(
        [jnp.where(first, in_mine, in_theirs), jnp.where(first, in_theirs, in_mine)], axis=1
    ).reshape(total_rows, channels)
    back_tokens = scatter_tok(in_part, F32)
    local_back = local_transform(back_tokens, table, lax.Precision.HIGHEST)
    rotated_product = cross(local_back, my_index) * root_scale * channel_signs[None, :]
    token_terms = jnp.sum(probe_signs * rotated_product, axis=0)
    pieces = gather_tok(token_terms.reshape(-1, LANES))
    pieces = pieces.reshape(lax.axis_size("tok"), channels // LANES, LANES)
    diagonal_estimate = jnp.sum(pieces, axis=0).reshape(channels) / total_rows
    return (rotated_product, diagonal_estimate)


def solution(mesh):
    placed = (
        P("tok", "ch"),
        P("tok", "ch"),
        P("ch"),
        P("ch", "tok"),
        P("ch", "tok"),
        P("tok", "ch"),
    )
    return jax.shard_map(
        on_device, mesh=mesh, in_specs=placed, out_specs=(P("tok", "ch"), P("ch")), check_vma=False
    )
```

profile of v0, /device:TPU:2, one launch (start us, length us, event | category | flops | bytes accessed | tf_op | source)
XLA Modules:
  0.0 309.4 jit_solution(1250894216051346519)
XLA Ops:
  7.2 0.8 add_convert_fusion
  8.0 1.0 multiply_convert_fusion.3
  9.2 1.2 collective-permute-done
  10.4 0.9 add_select_fusion.5
  11.2 2.0 collective-permute-start.1
  13.2 2.0 collective-permute-done.1
  15.2 3.4 %collective-permute-start.2 = (bf16[16,1024]{1,0:T(8,128)(2,1)S(1)}, bf16[16,1024]{1,0:T(8,128)(2,1)S(1)}, u32[]{:S(2)}, u32[]{:S(2)}) collective-permute-start(bf16[16,1024]{1,0:T(8,128)(2,1)S(1)} %add_select_fusion.4), channel_id=1, source_target_pairs={{0,4},{1,5},{2,6},{3,7},{4,0},{5,1},{6,2},{7,3},{8,12},{9,13},{10,... | collective-permute-start | bytes 98312 | tf_op jit(solution)/shard_map/ppermute | solution.py:23
  18.6 1.9 collective-permute-done.2
  20.5 6.9 %collective-permute-start.3 = (bf16[16,1024]{1,0:T(8,128)(2,1)S(1)}, bf16[16,1024]{1,0:T(8,128)(2,1)S(1)}, u32[]{:S(2)}, u32[]{:S(2)}) collective-permute-start(bf16[16,1024]{1,0:T(8,128)(2,1)S(1)} %add_select_fusion.3), channel_id=1, source_target_pairs={{0,8},{1,9},{2,10},{3,11},{4,12},{5,13},{6,14},{7,15},{8,0},{9,1},... | collective-permute-start | bytes 98312 | tf_op jit(solution)/shard_map/ppermute | solution.py:23
  27.4 1.6 broadcast_in_dim.10
  29.1 7.5 %all-to-all-start = ((bf16[16,16,1024]{2,1,0:T(8,128)(2,1)}), bf16[16,16,1024]{2,1,0:T(8,128)(2,1)}, u32[]{:S(2)}, u32[]{:S(2)}) async-start(bf16[16,16,1024]{2,1,0:T(8,128)(2,1)} %broadcast_in_dim.10), calls=%async_computation | async-start | bytes 1048576 | tf_op jit(solution)/shard_map/all_to_all | solution.py:54
  36.7 1.0 fusion.12
  37.8 7.6 %all-to-all-done = bf16[16,16,1024]{2,1,0:T(8,128)(2,1)} async-done(((bf16[16,16,1024]{2,1,0:T(8,128)(2,1)}), bf16[16,16,1024]{2,1,0:T(8,128)(2,1)}, u32[]{:S(2)}, u32[]{:S(2)}) %all-to-all-start) | async-done | bytes 524320 | tf_op jit(solution)/shard_map/all_to_all | solution.py:54
  45.4 3.2 %convolution_bitcast_fusion = f32[256,1,1664]{2,0,1:T(8,128)S(1)} fusion(bf16[256,1024]{1,0:T(8,128)(2,1)} %bitcast, bf16[1024,1664]{1,0:T(8,128)(2,1)} %param.11), kind=kOutput, calls=%fused_computation.1 | convolution fusion | flops 872415232 | bytes 5636096 | tf_op jit(solution)/shard_map/dot_general | solution.py:88
  48.7 2.2 convolution_bitcast_fusion.1
  50.8 1.9 pad_maximum_fusion
  52.9 0.8 broadcast_in_dim.11
  53.7 5.4 %all-to-all-start.1 = ((bf16[16,16,1024]{2,1,0:T(8,128)(2,1)}), bf16[16,16,1024]{2,1,0:T(8,128)(2,1)}, u32[]{:S(2)}, u32[]{:S(2)}) async-start(bf16[16,16,1024]{2,1,0:T(8,128)(2,1)} %broadcast_in_dim.11), calls=%async_computation.2 | async-start | bytes 1048576 | tf_op jit(solution)/shard_map/all_to_all | solution.py:54
  59.2 9.0 %all-to-all-done.1 = bf16[16,16,1024]{2,1,0:T(8,128)(2,1)} async-done(((bf16[16,16,1024]{2,1,0:T(8,128)(2,1)}), bf16[16,16,1024]{2,1,0:T(8,128)(2,1)}, u32[]{:S(2)}, u32[]{:S(2)}) %all-to-all-start.1) | async-done | bytes 524320 | tf_op jit(solution)/shard_map/all_to_all | solution.py:54
  68.1 1.1 constant_dynamic-slice_fusion.2
  69.2 2.6 convolution_convert_fusion
  73.4 1.2 copy-done.1
  75.3 32.4 %all_to_all.40 = bf16[8,16,3328]{2,1,0:T(8,128)(2,1)S(1)} all-to-all(bf16[8,16,3328]{2,1,0:T(8,128)(2,1)S(1)} %bitcast.71), channel_id=1, replica_groups={{0,2,4,6,8,10,12,14},{1,3,5,7,9,11,13,15},{16,18,20,22,24,26,28,30},{17..., dimensions={0} | all-to-all | bytes 1703936 | tf_op jit(solution)/shard_map/all_to_all | solution.py:83
  108.6 12.0 %reduce-scatter.2.cloned.1.call-done = f32[16,2,1664]{2,0,1:T(8,128)} async-done(((f32[256,2,1664]{2,0,1:T(8,128)}), f32[16,2,1664]{2,0,1:T(8,128)}) %reduce-scatter.2.cloned.1.call-update) | async-done | bytes 213008 | tf_op jit(solution)/shard_map/reduce_scatter | solution.py:107
  120.6 1.1 fusion.9
  121.7 17.1 %all_gather.6 = bf16[256,1664]{1,0:T(8,128)(2,1)S(1)} all-gather(bf16[16,1664]{1,0:T(8,128)(2,1)S(1)} %fusion.9), channel_id=1, replica_groups=mesh['tok'=16,'ch'=16] {'ch'}, dimensions={0}, use_global_device_ids=true | all-gather | bytes 905216 | tf_op jit(solution)/shard_map/all_gather | solution.py:124
  138.8 3.1 %fusion.15 = f32[256,1024]{1,0:T(8,128)S(1)} fusion(bf16[256,1664]{1,0:T(8,128)(2,1)S(1)} %all_gather.6, bf16[1664,1024]{1,0:T(8,128)(2,1)} %param.12), kind=kOutput, calls=%fused_computation.106 | convolution fusion | flops 872415232 | bytes 5308416 | tf_op jit(solution)/shard_map/dot_general | solution.py:88
  141.9 23.0 %all_to_all.41 = f32[16,16,1024]{2,1,0:T(8,128)} all-to-all(f32[16,16,1024]{2,1,0:T(8,128)S(1)} %bitcast.82), channel_id=1, replica_groups=mesh['tok'=16,'ch'=16] {'tok'}, dimensions={0} | all-to-all | bytes 2097152 | tf_op jit(solution)/shard_map/all_to_all | solution.py:60
  164.9 1.3 reduce_sum.55
  166.3 14.2 %all_to_all.42 = bf16[16,16,1024]{2,1,0:T(8,128)(2,1)S(1)} all-to-all(bf16[16,16,1024]{2,1,0:T(8,128)(2,1)S(1)} %broadcast_in_dim.12), channel_id=1, replica_groups=mesh['tok'=16,'ch'=16] {'tok'}, dimensions={0} | all-to-all | bytes 1048576 | tf_op jit(solution)/shard_map/all_to_all | solution.py:54
  180.5 3.2 %fusion.16 = f32[128,1664]{1,0:T(8,128)S(1)} fusion(bf16[128,1024]{1,0:T(8,128)(2,1)S(1)} %bitcast.81, bf16[1664,1024]{1,0:T(8,128)(2,1)} %param.12), kind=kOutput, calls=%fused_computation.107 | convolution fusion | flops 436207616 | bytes 4521984 | tf_op jit(solution)/shard_map/dot_general | solution.py:92
  184.0 2.4 collective-permute-done.5
  186.3 1.2 fusion
  187.6 21.8 %all_to_all.43 = bf16[8,16,1664]{2,1,0:T(8,128)(2,1)S(1)} all-to-all(bf16[8,16,1664]{2,1,0:T(8,128)(2,1)S(1)} %bitcast.79), channel_id=1, replica_groups={{0,2,4,6,8,10,12,14},{1,3,5,7,9,11,13,15},{16,18,20,22,24,26,28,30},{17..., dimensions={0} | all-to-all | bytes 851968 | tf_op jit(solution)/shard_map/all_to_all | solution.py:83
  209.5 28.2 %all_gather.7 = bf16[128,3328]{1,0:T(8,128)(2,1)} all-gather(bf16[16,3328]{1,0:T(8,128)(2,1)S(1)} %pad_maximum_fusion.3), channel_id=1, replica_groups={{0,2,4,6,8,10,12,14},{1,3,5,7,9,11,13,15},{16,18,20,22,24,26,28,30},{17..., dimensions={0}, use_global_device_ids=true | all-gather | bytes 958464 | tf_op jit(solution)/shard_map/all_gather | solution.py:131
  237.8 2.4 fusion.6
  240.1 2.2 convolution_add_fusion.2
  242.4 2.2 fusion.2
  244.6 2.2 broadcast_select_fusion.1
  247.0 21.5 %all_to_all.44 = f32[16,16,1024]{2,1,0:T(8,128)} all-to-all(f32[16,16,1024]{2,1,0:T(8,128)S(1)} %bitcast.70), channel_id=1, replica_groups=mesh['tok'=16,'ch'=16] {'tok'}, dimensions={0} | all-to-all | bytes 2097152 | tf_op jit(solution)/shard_map/all_to_all | solution.py:60
  268.4 1.3 reduce_sum.57
  269.9 1.0 fusion.17
  271.1 1.2 collective-permute-done.7
  272.4 4.3 %collective-permute-done.8 = f32[16,1024]{1,0:T(8,128)S(1)} collective-permute-done((f32[16,1024]{1,0:T(8,128)S(1)}, f32[16,1024]{1,0:T(8,128)S(1)}, u32[]{:S(2)}, u32[]{:S(2)}) %collective-permute-start.8) | collective-permute-done | bytes 65568 | tf_op jit(solution)/shard_map/ppermute | solution.py:23
  277.0 5.2 %collective-permute-done.9 = f32[16,1024]{1,0:T(8,128)S(1)} collective-permute-done((f32[16,1024]{1,0:T(8,128)S(1)}, f32[16,1024]{1,0:T(8,128)S(1)}, u32[]{:S(2)}, u32[]{:S(2)}) %collective-permute-start.9) | collective-permute-done | bytes 65568 | tf_op jit(solution)/shard_map/ppermute | solution.py:23
  282.3 1.7 collective-permute-start.10
  284.0 6.6 %collective-permute-done.10 = f32[16,1024]{1,0:T(8,128)S(1)} collective-permute-done((f32[16,1024]{1,0:T(8,128)S(1)}, f32[16,1024]{1,0:T(8,128)S(1)}, u32[]{:S(2)}, u32[]{:S(2)}) %collective-permute-start.10) | collective-permute-done | bytes 65568 | tf_op jit(solution)/shard_map/ppermute | solution.py:23
  291.2 10.7 %all_to_all.45 = f32[16,8,128]{2,1,0:T(8,128)S(1)} all-to-all(f32[16,8,128]{2,1,0:T(8,128)S(1)} %broadcast_in_dim.14), channel_id=1, replica_groups=mesh['tok'=16,'ch'=16] {'tok'}, dimensions={0} | all-to-all | bytes 131072 | tf_op jit(solution)/shard_map/all_to_all | solution.py:54
  (81 shorter events, 5.9 us)
Async XLA Ops:
  7.2 41.5 %copy-start = (bf16[1024,1664]{1,0:T(8,128)(2,1)S(1)}, bf16[1024,1664]{1,0:T(8,128)(2,1)}, u32[]{:S(2)}) copy-start(bf16[1024,1664]{1,0:T(8,128)(2,1)} %param.10) | copy-start | bytes 10223620
  9.1 1.3 collective-permute-start
  11.2 4.0 %collective-permute-start.1 = (bf16[16,1024]{1,0:T(8,128)(2,1)S(1)}, bf16[16,1024]{1,0:T(8,128)(2,1)S(1)}, u32[]{:S(2)}, u32[]{:S(2)}) collective-permute-start(bf16[16,1024]{1,0:T(8,128)(2,1)S(1)} %add_select_fusion.5), channel_id=1, source_target_pairs={{0,2},{1,3},{2,0},{3,1},{4,6},{5,7},{6,4},{7,5},{8,10},{9,11},{10,... | collective-permute-start | bytes 98312 | tf_op jit(solution)/shard_map/ppermute | solution.py:23
  15.2 5.3 %collective-permute-start.2 = (bf16[16,1024]{1,0:T(8,128)(2,1)S(1)}, bf16[16,1024]{1,0:T(8,128)(2,1)S(1)}, u32[]{:S(2)}, u32[]{:S(2)}) collective-permute-start(bf16[16,1024]{1,0:T(8,128)(2,1)S(1)} %add_select_fusion.4), channel_id=1, source_target_pairs={{0,4},{1,5},{2,6},{3,7},{4,0},{5,1},{6,2},{7,3},{8,12},{9,13},{10,... | collective-permute-start | bytes 98312 | tf_op jit(solution)/shard_map/ppermute | solution.py:23
  20.5 16.1 %collective-permute-start.3 = (bf16[16,1024]{1,0:T(8,128)(2,1)S(1)}, bf16[16,1024]{1,0:T(8,128)(2,1)S(1)}, u32[]{:S(2)}, u32[]{:S(2)}) collective-permute-start(bf16[16,1024]{1,0:T(8,128)(2,1)S(1)} %add_select_fusion.3), channel_id=1, source_target_pairs={{0,8},{1,9},{2,10},{3,11},{4,12},{5,13},{6,14},{7,15},{8,0},{9,1},... | collective-permute-start | bytes 98312 | tf_op jit(solution)/shard_map/ppermute | solution.py:23
  29.1 16.4 %all-to-all-start = ((bf16[16,16,1024]{2,1,0:T(8,128)(2,1)}), bf16[16,16,1024]{2,1,0:T(8,128)(2,1)}, u32[]{:S(2)}, u32[]{:S(2)}) async-start(bf16[16,16,1024]{2,1,0:T(8,128)(2,1)} %broadcast_in_dim.10), calls=%async_computation | async-start | bytes 1048576 | tf_op jit(solution)/shard_map/all_to_all | solution.py:54
  36.5 84.1 %reduce-scatter.2.cloned.1.call-start = ((), (), s32[]{:S(2)}) async-start(), calls=%async_computation.9 | async-start | bytes 3620864 | tf_op jit(solution)/shard_map/reduce_scatter | solution.py:107
  53.7 14.4 %all-to-all-start.1 = ((bf16[16,16,1024]{2,1,0:T(8,128)(2,1)}), bf16[16,16,1024]{2,1,0:T(8,128)(2,1)}, u32[]{:S(2)}, u32[]{:S(2)}) async-start(bf16[16,16,1024]{2,1,0:T(8,128)(2,1)} %broadcast_in_dim.11), calls=%async_computation.2 | async-start | bytes 1048576 | tf_op jit(solution)/shard_map/all_to_all | solution.py:54
  72.5 2.0 copy-start.1
  72.6 2.6 collective-permute-start.4
  166.3 20.1 %copy-start.3 = (bf16[1664,1024]{1,0:T(8,128)(2,1)S(1)}, bf16[1664,1024]{1,0:T(8,128)(2,1)}, u32[]{:S(2)}) copy-start(bf16[1664,1024]{1,0:T(8,128)(2,1)} %param.12) | copy-start | bytes 10223620
  183.7 25.8 %copy-start.4 = (f32[16,2,1664]{2,0,1:T(8,128)S(1)}, f32[16,2,1664]{2,0,1:T(8,128)}, u32[]{:S(2)}) copy-start(f32[16,2,1664]{2,0,1:T(8,128)} %reduce-scatter.2.cloned.1.call-done) | copy-start | bytes 638980
  183.7 2.6 collective-permute-start.5
  237.7 4.6 %collective-permute-start.6 = (bf16[128,3328]{1,0:T(8,128)(2,1)}, bf16[128,3328]{1,0:T(8,128)(2,1)}, u32[]{:S(2)}, u32[]{:S(2)}) collective-permute-start(bf16[128,3328]{1,0:T(8,128)(2,1)} %all_gather.7), channel_id=1, source_target_pairs={{0,1},{1,0},{2,3},{3,2},{4,5},{5,4},{6,7},{7,6},{8,9},{9,8},{10,11... | collective-permute-start | bytes 2555912 | tf_op jit(solution)/shard_map/ppermute | solution.py:23
  237.8 2.4 copy-start.2
  246.9 37.1 %copy-start.6 = (s32[1024]{0:T(1024)S(1)}, s32[1024]{0:T(1024)}, u32[]{:S(2)}) copy-start(s32[1024]{0:T(1024)} %param.9) | copy-start | bytes 12292
  246.9 43.7 %copy-start.5 = (s32[16,1024]{1,0:T(8,128)S(1)}, s32[16,1024]{1,0:T(8,128)}, u32[]{:S(2)}) copy-start(s32[16,1024]{1,0:T(8,128)} %param.8) | copy-start | bytes 196612
  271.0 1.3 collective-permute-start.7
  272.3 4.4 %collective-permute-start.8 = (f32[16,1024]{1,0:T(8,128)S(1)}, f32[16,1024]{1,0:T(8,128)S(1)}, u32[]{:S(2)}, u32[]{:S(2)}) collective-permute-start(f32[16,1024]{1,0:T(8,128)S(1)} %add_select_fusion.2), channel_id=1, source_target_pairs={{0,2},{1,3},{2,0},{3,1},{4,6},{5,7},{6,4},{7,5},{8,10},{9,11},{10,... | collective-permute-start | bytes 196616 | tf_op jit(solution)/shard_map/ppermute | solution.py:23
  276.7 5.6 %collective-permute-start.9 = (f32[16,1024]{1,0:T(8,128)S(1)}, f32[16,1024]{1,0:T(8,128)S(1)}, u32[]{:S(2)}, u32[]{:S(2)}) collective-permute-start(f32[16,1024]{1,0:T(8,128)S(1)} %add_select_fusion.1), channel_id=1, source_target_pairs={{0,4},{1,5},{2,6},{3,7},{4,0},{5,1},{6,2},{7,3},{8,12},{9,13},{10,... | collective-permute-start | bytes 196616 | tf_op jit(solution)/shard_map/ppermute | solution.py:23
  282.3 8.3 %collective-permute-start.10 = (f32[16,1024]{1,0:T(8,128)S(1)}, f32[16,1024]{1,0:T(8,128)S(1)}, u32[]{:S(2)}, u32[]{:S(2)}) collective-permute-start(f32[16,1024]{1,0:T(8,128)S(1)} %add_select_fusion), channel_id=1, source_target_pairs={{0,8},{1,9},{2,10},{3,11},{4,12},{5,13},{6,14},{7,15},{8,0},{9,1},... | collective-permute-start | bytes 196616 | tf_op jit(solution)/shard_map/ppermute | solution.py:23
Sparse Core Ops, SparseCore 0:
  52.9 67.6 reduce-scatter.1
where the time goes:
time: 311 us; the launch traced here: 309 us
  blocking collectives  169 us (54%)
  waiting for transfers between devices  53.5 us (17%)
  matrix products  28.7 us (9%)
  starting transfers between devices  27.9 us (9%)
  between operations  14.6 us (5%)
  other arithmetic  11.1 us (4%)
  local copies, waits for them, and re-layouts  4.86 us (2%)
    all_to_all x2, blocking collectives, scatter_ch(): lax.all_to_all(blocks, 'ch', 0, 0, tiled=True, axis_index_groups=chip_gro...  54.2 us
    all_to_all x2, blocking collectives, scatter_tok(): arrived = lax.all_to_all(blocks, 'tok', 0, 0, tiled=True)  44.5 us
    all_gather x1, blocking collectives, on_device(): lax.all_gather(back, 'ch', axis=0, tiled=True, axis_index_groups=chip_gro...  28.2 us
    all_to_all x2, blocking collectives, gather_tok(): return lax.all_to_all(copies, 'tok', 0, 0, tiled=True)  24.9 us
    ppermute x11, waiting for transfers between devices, swap(): return lax.ppermute(value, 'ch', pairs)  24.8 us
    all_gather x1, blocking collectives, on_device(): lax.all_gather(hidden_tan, 'ch', axis=0, tiled=True)  17.1 us
    all_to_all x2, waiting for transfers between devices, gather_tok(): return lax.all_to_all(copies, 'tok', 0, 0, tiled=True)  16.6 us
    ppermute x11, starting transfers between devices, swap(): return lax.ppermute(value, 'ch', pairs)  14.9 us
  transfers between devices with their start and end apart: 14, of which 11 were waited for; matrix products, arithmetic and copies ran while one was open for 5% of the time, Pallas kernels for 0%

commit v1 on v0

--- a/solution.py
+++ b/solution.py
@@ -121,7 +121,12 @@
     activated = gate_pre * sigmoid_gate
     slope_term = sigmoid_gate * (1.0 + gate_pre * (1.0 - sigmoid_gate))
     hidden_tan = (slope_term * gate_tan * up_pre + activated * up_tan).astype(BF16)
-    out_part = times(lax.all_gather(hidden_tan, "ch", axis=0, tiled=True), down_weight)
+    out_part = times(
+        jnp.concatenate(
+            lax.all_to_all(jnp.stack([hidden_tan] * lax.axis_size("ch")), "ch", 0, 0), axis=0
+        ),
+        down_weight,
+    )
     out_tangent = scatter_tok(out_part, F32).astype(BF16)
     all_out = gather_tok(out_tangent).reshape(total_rows, channels)
     back_hidden = scatter_ch(lambda rows: times_t(rows, down_weight), all_out, core, F32, BF16)

time: 311 us -> 323 us (1.039)
  blocking collectives: 169 us -> 180 us
    all_to_all x0 -> x1, blocking collectives: none -> 29.7 us  [on_device(): lax.all_to_all(jnp.stack([hidden_tan] * lax.axis_size('ch')), 'ch', 0, 0)]
    all_gather x1 -> x0, blocking collectives: 17.1 us -> none  [on_device(): lax.all_gather(hidden_tan, 'ch', axis=0, tiled=True)]
    all_to_all x2, blocking collectives: 54.2 us -> 50.8 us  [scatter_ch(): lax.all_to_all(blocks, 'ch', 0, 0, tiled=True, axis_index_groups=chip_gro...]
where the time goes in v1:
time: 323 us; the launch traced here: 321 us
  blocking collectives  180 us (56%)
  waiting for transfers between devices  54 us (17%)
  matrix products  28.7 us (9%)
  starting transfers between devices  27.8 us (9%)
  between operations  14.6 us (5%)
  other arithmetic  11.1 us (3%)
  local copies, waits for them, and re-layouts  4.92 us (2%)
    all_to_all x2, blocking collectives, scatter_ch(): lax.all_to_all(blocks, 'ch', 0, 0, tiled=True, axis_index_groups=chip_gro...  50.8 us
    all_to_all x2, blocking collectives, scatter_tok(): arrived = lax.all_to_all(blocks, 'tok', 0, 0, tiled=True)  45.9 us
    all_to_all x1, blocking collectives, on_device(): lax.all_to_all(jnp.stack([hidden_tan] * lax.axis_size('ch')), 'ch', 0, 0)  29.7 us
    all_gather x1, blocking collectives, on_device(): lax.all_gather(back, 'ch', axis=0, tiled=True, axis_index_groups=chip_gro...  28.3 us
    all_to_all x2, blocking collectives, gather_tok(): return lax.all_to_all(copies, 'tok', 0, 0, tiled=True)  25.6 us
    ppermute x11, waiting for transfers between devices, swap(): return lax.ppermute(value, 'ch', pairs)  25.3 us
    all_to_all x2, waiting for transfers between devices, gather_tok(): return lax.all_to_all(copies, 'tok', 0, 0, tiled=True)  16.6 us
    ppermute x11, starting transfers between devices, swap(): return lax.ppermute(value, 'ch', pairs)  14.9 us
  transfers between devices with their start and end apart: 14, of which 11 were waited for; matrix products, arithmetic and copies ran while one was open for 5% of the time, Pallas kernels for 0%

profile of v1, /device:TPU:2, one launch (start us, length us, event | category | flops | bytes accessed | tf_op | source)
XLA Modules:
  0.0 321.4 jit_solution(9788505599749150938)
XLA Ops:
  7.2 0.8 add_convert_fusion
  8.0 1.0 multiply_convert_fusion.3
  9.2 1.2 collective-permute-done
  10.4 0.9 add_select_fusion.5
  11.2 2.0 collective-permute-start.1
  13.2 2.0 collective-permute-done.1
  15.2 3.4 %collective-permute-start.2 = (bf16[16,1024]{1,0:T(8,128)(2,1)S(1)}, bf16[16,1024]{1,0:T(8,128)(2,1)S(1)}, u32[]{:S(2)}, u32[]{:S(2)}) collective-permute-start(bf16[16,1024]{1,0:T(8,128)(2,1)S(1)} %add_select_fusion.4), channel_id=1, source_target_pairs={{0,4},{1,5},{2,6},{3,7},{4,0},{5,1},{6,2},{7,3},{8,12},{9,13},{10,... | collective-permute-start | bytes 98312 | tf_op jit(solution)/shard_map/ppermute | solution.py:23
  18.6 1.9 collective-permute-done.2
  20.5 6.9 %collective-permute-start.3 = (bf16[16,1024]{1,0:T(8,128)(2,1)S(1)}, bf16[16,1024]{1,0:T(8,128)(2,1)S(1)}, u32[]{:S(2)}, u32[]{:S(2)}) collective-permute-start(bf16[16,1024]{1,0:T(8,128)(2,1)S(1)} %add_select_fusion.3), channel_id=1, source_target_pairs={{0,8},{1,9},{2,10},{3,11},{4,12},{5,13},{6,14},{7,15},{8,0},{9,1},... | collective-permute-start | bytes 98312 | tf_op jit(solution)/shard_map/ppermute | solution.py:23
  27.4 1.6 broadcast_in_dim.10
  29.1 7.5 %all-to-all-start = ((bf16[16,16,1024]{2,1,0:T(8,128)(2,1)}), bf16[16,16,1024]{2,1,0:T(8,128)(2,1)}, u32[]{:S(2)}, u32[]{:S(2)}) async-start(bf16[16,16,1024]{2,1,0:T(8,128)(2,1)} %broadcast_in_dim.10), calls=%async_computation | async-start | bytes 1048576 | tf_op jit(solution)/shard_map/all_to_all | solution.py:54
  36.7 1.0 fusion.14
  37.8 7.6 %all-to-all-done = bf16[16,16,1024]{2,1,0:T(8,128)(2,1)} async-done(((bf16[16,16,1024]{2,1,0:T(8,128)(2,1)}), bf16[16,16,1024]{2,1,0:T(8,128)(2,1)}, u32[]{:S(2)}, u32[]{:S(2)}) %all-to-all-start) | async-done | bytes 524320 | tf_op jit(solution)/shard_map/all_to_all | solution.py:54
  45.4 3.2 %convolution_bitcast_fusion = f32[256,1,1664]{2,0,1:T(8,128)S(1)} fusion(bf16[256,1024]{1,0:T(8,128)(2,1)} %bitcast, bf16[1024,1664]{1,0:T(8,128)(2,1)} %param.11), kind=kOutput, calls=%fused_computation.3 | convolution fusion | flops 872415232 | bytes 5636096 | tf_op jit(solution)/shard_map/dot_general | solution.py:88
  48.7 2.2 convolution_bitcast_fusion.1
  50.8 1.9 pad_maximum_fusion
  52.9 0.8 broadcast_in_dim.11
  53.7 5.4 %all-to-all-start.1 = ((bf16[16,16,1024]{2,1,0:T(8,128)(2,1)}), bf16[16,16,1024]{2,1,0:T(8,128)(2,1)}, u32[]{:S(2)}, u32[]{:S(2)}) async-start(bf16[16,16,1024]{2,1,0:T(8,128)(2,1)} %broadcast_in_dim.11), calls=%async_computation.2 | async-start | bytes 1048576 | tf_op jit(solution)/shard_map/all_to_all | solution.py:54
  59.2 9.0 %all-to-all-done.1 = bf16[16,16,1024]{2,1,0:T(8,128)(2,1)} async-done(((bf16[16,16,1024]{2,1,0:T(8,128)(2,1)}), bf16[16,16,1024]{2,1,0:T(8,128)(2,1)}, u32[]{:S(2)}, u32[]{:S(2)}) %all-to-all-start.1) | async-done | bytes 524320 | tf_op jit(solution)/shard_map/all_to_all | solution.py:54
  68.1 1.1 constant_dynamic-slice_fusion.2
  69.2 2.6 convolution_convert_fusion
  73.4 1.2 copy-done.1
  75.3 32.4 %all_to_all.45 = bf16[8,16,3328]{2,1,0:T(8,128)(2,1)S(1)} all-to-all(bf16[8,16,3328]{2,1,0:T(8,128)(2,1)S(1)} %bitcast.72), channel_id=1, replica_groups={{0,2,4,6,8,10,12,14},{1,3,5,7,9,11,13,15},{16,18,20,22,24,26,28,30},{17..., dimensions={0} | all-to-all | bytes 1703936 | tf_op jit(solution)/shard_map/all_to_all | solution.py:83
  108.6 12.0 %reduce-scatter.2.cloned.1.call-done = f32[16,2,1664]{2,0,1:T(8,128)} async-done(((f32[256,2,1664]{2,0,1:T(8,128)}), f32[16,2,1664]{2,0,1:T(8,128)}) %reduce-scatter.2.cloned.1.call-update) | async-done | bytes 213008 | tf_op jit(solution)/shard_map/reduce_scatter | solution.py:107
  120.6 1.1 fusion.11
  121.8 29.7 %all_to_all.46 = bf16[16,16,1664]{2,1,0:T(8,128)(2,1)S(1)} all-to-all(bf16[16,16,1664]{2,1,0:T(8,128)(2,1)S(1)} %stack.13), channel_id=1, replica_groups=mesh['tok'=16,'ch'=16] {'ch'}, dimensions={0} | all-to-all | bytes 1703936 | tf_op jit(solution)/shard_map/all_to_all | solution.py:126
  151.5 3.1 fusion
  154.7 24.5 %all_to_all.47 = f32[16,16,1024]{2,1,0:T(8,128)} all-to-all(f32[16,16,1024]{2,1,0:T(8,128)S(1)} %fusion), channel_id=1, replica_groups=mesh['tok'=16,'ch'=16] {'tok'}, dimensions={0} | all-to-all | bytes 2097152 | tf_op jit(solution)/shard_map/all_to_all | solution.py:60
  179.1 1.3 reduce_sum.55
  180.5 14.9 %all_to_all.48 = bf16[16,16,1024]{2,1,0:T(8,128)(2,1)S(1)} all-to-all(bf16[16,16,1024]{2,1,0:T(8,128)(2,1)S(1)} %broadcast_in_dim.12), channel_id=1, replica_groups=mesh['tok'=16,'ch'=16] {'tok'}, dimensions={0} | all-to-all | bytes 1048576 | tf_op jit(solution)/shard_map/all_to_all | solution.py:54
  195.4 3.2 fusion.17
  198.9 2.4 collective-permute-done.5
  201.2 1.2 fusion.2
  202.5 18.4 %all_to_all.49 = bf16[8,16,1664]{2,1,0:T(8,128)(2,1)S(1)} all-to-all(bf16[8,16,1664]{2,1,0:T(8,128)(2,1)S(1)} %bitcast.80), channel_id=1, replica_groups={{0,2,4,6,8,10,12,14},{1,3,5,7,9,11,13,15},{16,18,20,22,24,26,28,30},{17..., dimensions={0} | all-to-all | bytes 851968 | tf_op jit(solution)/shard_map/all_to_all | solution.py:83
  221.0 28.3 %all_gather.3 = bf16[128,3328]{1,0:T(8,128)(2,1)} all-gather(bf16[16,3328]{1,0:T(8,128)(2,1)S(1)} %pad_maximum_fusion.3), channel_id=1, replica_groups={{0,2,4,6,8,10,12,14},{1,3,5,7,9,11,13,15},{16,18,20,22,24,26,28,30},{17..., dimensions={0}, use_global_device_ids=true | all-gather | bytes 958464 | tf_op jit(solution)/shard_map/all_gather | solution.py:136
  249.3 2.4 fusion.8
  251.7 2.2 convolution_add_fusion.2
  254.0 2.2 fusion.4
  256.2 2.2 broadcast_select_fusion.1
  258.6 21.4 %all_to_all.50 = f32[16,16,1024]{2,1,0:T(8,128)} all-to-all(f32[16,16,1024]{2,1,0:T(8,128)S(1)} %bitcast.71), channel_id=1, replica_groups=mesh['tok'=16,'ch'=16] {'tok'}, dimensions={0} | all-to-all | bytes 2097152 | tf_op jit(solution)/shard_map/all_to_all | solution.py:60
  280.0 1.3 reduce_sum.57
  281.4 1.0 fusion.18
  282.6 1.2 collective-permute-done.7
  284.0 4.3 %collective-permute-done.8 = f32[16,1024]{1,0:T(8,128)S(1)} collective-permute-done((f32[16,1024]{1,0:T(8,128)S(1)}, f32[16,1024]{1,0:T(8,128)S(1)}, u32[]{:S(2)}, u32[]{:S(2)}) %collective-permute-start.8) | collective-permute-done | bytes 65568 | tf_op jit(solution)/shard_map/ppermute | solution.py:23
  288.6 5.2 %collective-permute-done.9 = f32[16,1024]{1,0:T(8,128)S(1)} collective-permute-done((f32[16,1024]{1,0:T(8,128)S(1)}, f32[16,1024]{1,0:T(8,128)S(1)}, u32[]{:S(2)}, u32[]{:S(2)}) %collective-permute-start.9) | collective-permute-done | bytes 65568 | tf_op jit(solution)/shard_map/ppermute | solution.py:23
  293.8 1.6 collective-permute-start.10
  295.5 7.1 %collective-permute-done.10 = f32[16,1024]{1,0:T(8,128)S(1)} collective-permute-done((f32[16,1024]{1,0:T(8,128)S(1)}, f32[16,1024]{1,0:T(8,128)S(1)}, u32[]{:S(2)}, u32[]{:S(2)}) %collective-permute-start.10) | collective-permute-done | bytes 65568 | tf_op jit(solution)/shard_map/ppermute | solution.py:23
  303.3 10.7 %all_to_all.51 = f32[16,8,128]{2,1,0:T(8,128)S(1)} all-to-all(f32[16,8,128]{2,1,0:T(8,128)S(1)} %broadcast_in_dim.14), channel_id=1, replica_groups=mesh['tok'=16,'ch'=16] {'tok'}, dimensions={0} | all-to-all | bytes 131072 | tf_op jit(solution)/shard_map/all_to_all | solution.py:54
  (82 shorter events, 5.9 us)
Async XLA Ops:
  7.2 41.5 %copy-start = (bf16[1024,1664]{1,0:T(8,128)(2,1)S(1)}, bf16[1024,1664]{1,0:T(8,128)(2,1)}, u32[]{:S(2)}) copy-start(bf16[1024,1664]{1,0:T(8,128)(2,1)} %param.10) | copy-start | bytes 10223620
  9.1 1.3 collective-permute-start
  11.2 4.0 %collective-permute-start.1 = (bf16[16,1024]{1,0:T(8,128)(2,1)S(1)}, bf16[16,1024]{1,0:T(8,128)(2,1)S(1)}, u32[]{:S(2)}, u32[]{:S(2)}) collective-permute-start(bf16[16,1024]{1,0:T(8,128)(2,1)S(1)} %add_select_fusion.5), channel_id=1, source_target_pairs={{0,2},{1,3},{2,0},{3,1},{4,6},{5,7},{6,4},{7,5},{8,10},{9,11},{10,... | collective-permute-start | bytes 98312 | tf_op jit(solution)/shard_map/ppermute | solution.py:23
  15.2 5.3 %collective-permute-start.2 = (bf16[16,1024]{1,0:T(8,128)(2,1)S(1)}, bf16[16,1024]{1,0:T(8,128)(2,1)S(1)}, u32[]{:S(2)}, u32[]{:S(2)}) collective-permute-start(bf16[16,1024]{1,0:T(8,128)(2,1)S(1)} %add_select_fusion.4), channel_id=1, source_target_pairs={{0,4},{1,5},{2,6},{3,7},{4,0},{5,1},{6,2},{7,3},{8,12},{9,13},{10,... | collective-permute-start | bytes 98312 | tf_op jit(solution)/shard_map/ppermute | solution.py:23
  20.5 16.1 %collective-permute-start.3 = (bf16[16,1024]{1,0:T(8,128)(2,1)S(1)}, bf16[16,1024]{1,0:T(8,128)(2,1)S(1)}, u32[]{:S(2)}, u32[]{:S(2)}) collective-permute-start(bf16[16,1024]{1,0:T(8,128)(2,1)S(1)} %add_select_fusion.3), channel_id=1, source_target_pairs={{0,8},{1,9},{2,10},{3,11},{4,12},{5,13},{6,14},{7,15},{8,0},{9,1},... | collective-permute-start | bytes 98312 | tf_op jit(solution)/shard_map/ppermute | solution.py:23
  29.1 16.4 %all-to-all-start = ((bf16[16,16,1024]{2,1,0:T(8,128)(2,1)}), bf16[16,16,1024]{2,1,0:T(8,128)(2,1)}, u32[]{:S(2)}, u32[]{:S(2)}) async-start(bf16[16,16,1024]{2,1,0:T(8,128)(2,1)} %broadcast_in_dim.10), calls=%async_computation | async-start | bytes 1048576 | tf_op jit(solution)/shard_map/all_to_all | solution.py:54
  36.5 84.1 %reduce-scatter.2.cloned.1.call-start = ((), (), s32[]{:S(2)}) async-start(), calls=%async_computation.10 | async-start | bytes 3620864 | tf_op jit(solution)/shard_map/reduce_scatter | solution.py:107
  53.7 14.4 %all-to-all-start.1 = ((bf16[16,16,1024]{2,1,0:T(8,128)(2,1)}), bf16[16,16,1024]{2,1,0:T(8,128)(2,1)}, u32[]{:S(2)}, u32[]{:S(2)}) async-start(bf16[16,16,1024]{2,1,0:T(8,128)(2,1)} %broadcast_in_dim.11), calls=%async_computation.2 | async-start | bytes 1048576 | tf_op jit(solution)/shard_map/all_to_all | solution.py:54
  72.5 2.0 copy-start.1
  72.6 2.6 collective-permute-start.4
  180.5 20.8 %copy-start.3 = (bf16[1664,1024]{1,0:T(8,128)(2,1)S(1)}, bf16[1664,1024]{1,0:T(8,128)(2,1)}, u32[]{:S(2)}) copy-start(bf16[1664,1024]{1,0:T(8,128)(2,1)} %param.12) | copy-start | bytes 10223620
  198.6 22.3 %copy-start.4 = (f32[16,2,1664]{2,0,1:T(8,128)S(1)}, f32[16,2,1664]{2,0,1:T(8,128)}, u32[]{:S(2)}) copy-start(f32[16,2,1664]{2,0,1:T(8,128)} %reduce-scatter.2.cloned.1.call-done) | copy-start | bytes 638980
  198.6 2.6 collective-permute-start.5
  249.3 4.6 %collective-permute-start.6 = (bf16[128,3328]{1,0:T(8,128)(2,1)}, bf16[128,3328]{1,0:T(8,128)(2,1)}, u32[]{:S(2)}, u32[]{:S(2)}) collective-permute-start(bf16[128,3328]{1,0:T(8,128)(2,1)} %all_gather.3), channel_id=1, source_target_pairs={{0,1},{1,0},{2,3},{3,2},{4,5},{5,4},{6,7},{7,6},{8,9},{9,8},{10,11... | collective-permute-start | bytes 2555912 | tf_op jit(solution)/shard_map/ppermute | solution.py:23
  249.3 2.4 copy-start.2
  258.5 37.0 %copy-start.6 = (s32[1024]{0:T(1024)S(1)}, s32[1024]{0:T(1024)}, u32[]{:S(2)}) copy-start(s32[1024]{0:T(1024)} %param.9) | copy-start | bytes 12292
  258.5 44.1 %copy-start.5 = (s32[16,1024]{1,0:T(8,128)S(1)}, s32[16,1024]{1,0:T(8,128)}, u32[]{:S(2)}) copy-start(s32[16,1024]{1,0:T(8,128)} %param.8) | copy-start | bytes 196612
  282.5 1.3 collective-permute-start.7
  283.9 4.4 %collective-permute-start.8 = (f32[16,1024]{1,0:T(8,128)S(1)}, f32[16,1024]{1,0:T(8,128)S(1)}, u32[]{:S(2)}, u32[]{:S(2)}) collective-permute-start(f32[16,1024]{1,0:T(8,128)S(1)} %add_select_fusion.2), channel_id=1, source_target_pairs={{0,2},{1,3},{2,0},{3,1},{4,6},{5,7},{6,4},{7,5},{8,10},{9,11},{10,... | collective-permute-start | bytes 196616 | tf_op jit(solution)/shard_map/ppermute | solution.py:23
  288.3 5.6 %collective-permute-start.9 = (f32[16,1024]{1,0:T(8,128)S(1)}, f32[16,1024]{1,0:T(8,128)S(1)}, u32[]{:S(2)}, u32[]{:S(2)}) collective-permute-start(f32[16,1024]{1,0:T(8,128)S(1)} %add_select_fusion.1), channel_id=1, source_target_pairs={{0,4},{1,5},{2,6},{3,7},{4,0},{5,1},{6,2},{7,3},{8,12},{9,13},{10,... | collective-permute-start | bytes 196616 | tf_op jit(solution)/shard_map/ppermute | solution.py:23
  293.8 8.8 %collective-permute-start.10 = (f32[16,1024]{1,0:T(8,128)S(1)}, f32[16,1024]{1,0:T(8,128)S(1)}, u32[]{:S(2)}, u32[]{:S(2)}) collective-permute-start(f32[16,1024]{1,0:T(8,128)S(1)} %add_select_fusion), channel_id=1, source_target_pairs={{0,8},{1,9},{2,10},{3,11},{4,12},{5,13},{6,14},{7,15},{8,0},{9,1},... | collective-permute-start | bytes 196616 | tf_op jit(solution)/shard_map/ppermute | solution.py:23
Sparse Core Ops, SparseCore 0:
  52.9 67.6 reduce-scatter.1
